TPU v7x, 512 devices: a whole 4x8x8 slice. The times are simulated.
512 devices in a mesh: patch: 64 (over y, z), visit: 8 (over x, core).
Axes of the slice: x: 4, y: 8, z: 8, core: 2. Of those that a mesh axis runs over, the one named last changes fastest.
Arguments:
- stamps: bfloat16 [8, 8192, 32, 128], P('visit', 'patch'), may hold values from -6 to 6
- coefs: bfloat16 [8, 8192, 64], P('visit', 'patch'), may hold values from -0.75 to 0.75
- basis: bfloat16 [8, 64, 21, 21], P('visit', 'patch'), may hold values from -0.29882812 to 0.29882812
- taps: bfloat16 [8, 8192, 8], P('visit', 'patch'), may hold values from 0.049804688 to 0.59765625
- weights: bfloat16 [8, 8192], P('visit', 'patch'), may hold values from 0.19921875 to 5
- target: int32 [8, 8192, 1], P('visit', 'patch'), may hold values from 0 to 63; in each aligned block of 128 rows (0 to 127, 128 to 255, ..., all dimensions but the last counted through in order) at most 4 rows name the same one
- row_offset: int32 [8, 8192], P('visit', 'patch'), may hold values from 0 to 223
- col_offset: int32 [8, 8192], P('visit', 'patch'), may hold values from 0 to 127
Outputs:
- coadd: float32 [64, 256, 256], P('patch', 'visit')
- depth_map: float32 [64, 256, 256], P('patch', 'visit')
Inputs may be any that keep to these rules, and one draw needn't show every extreme that they name: `target`: among the rows of one device no patch is named more than 4 times, a bound that some block reaches.
All inputs are finite; a program needn't handle non-finite values.
Results may differ from a plain program's by a relative error of at most 0.0057.
Values may be sent and summed in bfloat16 or wider, within the bound.
No kernel may reach another device: no remote copies, remote signals or barrier semaphores. Data moves between devices by JAX's collectives and lax.ppermute only.
A program may use at most 64 MiB of HBM per device.

v0:
```python
import jax
import jax.numpy as jnp
from jax import lax
from jax.sharding import PartitionSpec as P

PATCH_ROWS = 256
PATCH_COLS = 256


def make_kernels(coefficients, basis_set):
    term_count = basis_set.shape[0]
    kernel_size = basis_set.shape[1]
    flat = jnp.dot(
        coefficients,
        basis_set.reshape(term_count, kernel_size * kernel_size),
        preferred_element_type=jnp.float32,
    )
    return flat.astype(jnp.bfloat16).reshape(coefficients.shape[0], kernel_size, kernel_size)


def convolve(pixels, kernels):
    kernel_size = kernels.shape[1]
    kernel_reach = kernel_size // 2
    height = pixels.shape[1]
    breadth = pixels.shape[2]
    padded = jnp.pad(pixels, ((0, 0), (0, 0), (kernel_reach, kernel_reach)))
    shifted = jnp.stack(
        [
            padded[:, :, column_shift : column_shift + breadth]
            for column_shift in range(kernel_size)
        ],
        axis=1,
    )
    offsets = (
        jnp.arange(height, dtype=jnp.int32)[None, :]
        - jnp.arange(height, dtype=jnp.int32)[:, None]
        + kernel_reach
    )
    onehot = (
        offsets[None, :, :] == jnp.arange(kernel_size, dtype=jnp.int32)[:, None, None]
    ).astype(jnp.bfloat16)
    toeplitz = jnp.einsum(
        "nab,aij->nbij", kernels, onehot, preferred_element_type=jnp.float32
    ).astype(jnp.bfloat16)
    result = jnp.einsum("nbik,nbkj->nij", toeplitz, shifted, preferred_element_type=jnp.float32)
    return result.astype(jnp.bfloat16)


def resample(convolved, tap_values, scale, row_start, col_start):
    height = convolved.shape[1]
    breadth = convolved.shape[2]
    column_gap = (
        jnp.arange(PATCH_COLS, dtype=jnp.int32)[None, :, None]
        - col_start[:, None, None]
        - jnp.arange(breadth, dtype=jnp.int32)[None, None, :]
        + 1
    )
    row_gap = (
        jnp.arange(PATCH_ROWS, dtype=jnp.int32)[None, :, None]
        - row_start[:, None, None]
        - jnp.arange(height, dtype=jnp.int32)[None, None, :]
        + 1
    )
    column_sum = jnp.zeros(column_gap.shape, jnp.float32)
    row_sum = jnp.zeros(row_gap.shape, jnp.float32)
    for tap_index in range(4):
        column_sum = column_sum + jnp.where(
            column_gap == tap_index,
            tap_values[:, 4 + tap_index].astype(jnp.float32)[:, None, None],
            0.0,
        )
        row_sum = row_sum + jnp.where(
            row_gap == tap_index, tap_values[:, tap_index].astype(jnp.float32)[:, None, None], 0.0
        )
    column_map = column_sum.astype(jnp.bfloat16)
    row_map = (scale.astype(jnp.float32)[:, None, None] * row_sum).astype(jnp.bfloat16)
    spread = jnp.einsum(
        "nij,ncj->nic", convolved, column_map, preferred_element_type=jnp.float32
    ).astype(jnp.bfloat16)
    return (row_map, column_map, spread)


def accumulate(pixels, extras, starts, full_basis):
    block_size = 8
    block_count = pixels.shape[0] // block_size
    term_count = full_basis.shape[0]
    blocks = (
        pixels.reshape(block_count, block_size, pixels.shape[1], pixels.shape[2]),
        extras.reshape(block_count, block_size, extras.shape[1]),
        starts.reshape(block_count, block_size, 2),
    )

    def update(state, block):
        numerator, depth_map = state
        convolved, extra_block, start_block = block
        convolved = convolve(convolved, make_kernels(extra_block[:, :term_count], full_basis))
        extra_block = extra_block[:, term_count:]
        row_map, column_map, spread = resample(
            convolved, extra_block[:, :8], extra_block[:, 8], start_block[:, 0], start_block[:, 1]
        )
        numerator = numerator + jnp.einsum(
            "nri,nic->rc", row_map, spread, preferred_element_type=jnp.float32
        )
        row_weight = jnp.sum(row_map.astype(jnp.float32), axis=2)
        column_weight = jnp.sum(column_map.astype(jnp.float32), axis=2)
        depth_map = depth_map + jnp.dot(
            row_weight.T, column_weight, precision=lax.Precision.HIGHEST
        )
        return ((numerator, depth_map), None)

    initial = (
        jnp.zeros((PATCH_ROWS, PATCH_COLS), jnp.float32),
        jnp.zeros((PATCH_ROWS, PATCH_COLS), jnp.float32),
    )
    final_state, unused = lax.scan(update, initial, blocks)
    return final_state


def per_device(stamps, coefs, basis, taps, weights, target, row_offset, col_offset):
    peer_count = lax.axis_size("patch")
    stamp_count = stamps.shape[1]
    height = stamps.shape[2]
    breadth = stamps.shape[3]
    slot_count = 2 * stamp_count // peer_count
    full_basis = lax.all_gather(basis[0], "patch", axis=0, tiled=True)
    destination = target[0, :, 0]
    position = jnp.arange(stamp_count, dtype=jnp.int32)
    earlier = (destination[None, :] == destination[:, None]) & (
        position[None, :] < position[:, None]
    )
    standing = jnp.sum(earlier.astype(jnp.int32), axis=1)
    placement = destination * slot_count + standing
    chooser = placement[None, :] == jnp.arange(peer_count * slot_count, dtype=jnp.int32)[:, None]
    select = chooser.astype(jnp.bfloat16)

    def pack(values):
        packed = jnp.dot(select, values, preferred_element_type=jnp.float32).astype(jnp.bfloat16)
        return packed.reshape(peer_count, slot_count, values.shape[1])

    starts = jnp.stack([row_offset[0], col_offset[0]], axis=1)
    packed_starts = jnp.sum(jnp.where(chooser[:, :, None], starts[None, :, :], 0), axis=1).reshape(
        peer_count, slot_count, 2
    )
    total_slots = peer_count * slot_count
    extras = jnp.concatenate([coefs[0], taps[0], weights[0][:, None]], axis=1)
    packed_pixels = pack(stamps[0].reshape(stamp_count, height * breadth))
    packed_extras = pack(extras)
    got_pixels, got_extras, got_starts = (
        lax.all_to_all(packed_pixels, "patch", split_axis=0, concat_axis=0, tiled=True),
        lax.all_to_all(packed_extras, "patch", split_axis=0, concat_axis=0, tiled=True),
        lax.all_to_all(packed_starts, "patch", split_axis=0, concat_axis=0, tiled=True),
    )
    numerator, depth_map = accumulate(
        got_pixels.reshape(total_slots, height, breadth),
        got_extras.reshape(total_slots, got_extras.shape[2]),
        got_starts.reshape(total_slots, 2),
        full_basis,
    )
    numerator, depth_map = (
        lax.psum_scatter(numerator, "visit", scatter_dimension=0, tiled=True),
        lax.psum_scatter(depth_map, "visit", scatter_dimension=0, tiled=True),
    )
    coadd = numerator / (1.0 + depth_map)
    return (coadd[None], depth_map[None])


def solution(mesh):
    placed = (
        P("visit", "patch", None, None),
        P("visit", "patch", None),
        P("visit", "patch", None, None),
        P("visit", "patch", None),
        P("visit", "patch"),
        P("visit", "patch", None),
        P("visit", "patch"),
        P("visit", "patch"),
    )
    return jax.shard_map(
        per_device,
        mesh=mesh,
        in_specs=placed,
        out_specs=(P("patch", "visit", None), P("patch", "visit", None)),
        check_vma=False,
    )
```

profile of v0, /device:TPU:8, one launch (start us, length us, event | category | flops | bytes accessed | tf_op | source)
XLA Modules:
  0.0 502.9 jit_solution(15867285318595806077)
XLA Ops:
  7.2 0.9 convert_reduce_fusion.2
  10.4 16.6 %all-to-all-start.1 = ((s32[64,4,2]{1,2,0:T(2,128)}), s32[64,4,2]{1,2,0:T(2,128)S(1)}, u32[]{:S(2)}, u32[]{:S(2)}) async-start(s32[64,4,2]{1,2,0:T(2,128)} %copy.93), calls=%async_computation.1 | async-start | bytes 131072 | tf_op jit(solution)/shard_map/all_to_all | solution.py:151
  27.0 2.0 convolution_convert_fusion.3
  28.9 2.2 reshape.221
  31.2 7.1 %all-to-all-done.1 = s32[64,4,2]{1,2,0:T(2,128)S(1)} async-done(((s32[64,4,2]{1,2,0:T(2,128)}), s32[64,4,2]{1,2,0:T(2,128)S(1)}, u32[]{:S(2)}, u32[]{:S(2)}) %all-to-all-start.1) | async-done | bytes 2080 | tf_op jit(solution)/shard_map/all_to_all | solution.py:151
  38.3 5.7 %all-to-all-start.2 = ((bf16[64,4,4096]{2,1,0:T(4,128)(2,1)}), bf16[64,4,4096]{2,1,0:T(4,128)(2,1)S(1)}, u32[]{:S(2)}, u32[]{:S(2)}) async-start(bf16[64,4,4096]{2,1,0:T(4,128)(2,1)} %reshape.221), calls=%async_computation.2 | async-start | bytes 4194304 | tf_op jit(solution)/shard_map/all_to_all | solution.py:149
  45.0 50.3 %all-to-all-done.2 = bf16[64,4,4096]{2,1,0:T(4,128)(2,1)S(1)} async-done(((bf16[64,4,4096]{2,1,0:T(4,128)(2,1)}), bf16[64,4,4096]{2,1,0:T(4,128)(2,1)S(1)}, u32[]{:S(2)}, u32[]{:S(2)}) %all-to-all-start.2) | async-done | bytes 2097184 | tf_op jit(solution)/shard_map/all_to_all | solution.py:149
  95.3 12.5 %all-to-all-start = ((bf16[64,4,73]{2,1,0:T(4,128)(2,1)}), bf16[64,4,73]{2,1,0:T(4,128)(2,1)S(1)}, u32[]{:S(2)}, u32[]{:S(2)}) async-start(bf16[64,4,73]{2,1,0:T(4,128)(2,1)} %bitcast.4), calls=%async_computation | async-start | bytes 131072 | tf_op jit(solution)/shard_map/all_to_all | solution.py:150
  107.9 49.5 %all-gather = bf16[64,1,21,21]{3,2,1,0:T(8,128)(2,1)S(1)} all-gather(bf16[1,1,21,21]{3,2,1,0:T(8,128)(2,1)S(1)} %copy-done.3), channel_id=2, replica_groups=mesh['patch'=64,'visit'=8] {'patch'}, dimensions={0}, use_global_device_ids=true | all-gather | bytes 57330 | tf_op jit(solution)/shard_map/all_gather | solution.py:125
  157.8 3.2 reshape_reshape.11
  161.0 261.2 %while.16 = (s32[]{:T(128)}, f32[256,256]{1,0:T(8,128)S(1)}, f32[256,256]{1,0:T(8,128)S(1)}, bf16[32,8,73]{2,1,0:T(8,128)(2,1)S(1)}, s32[32,8,2]{1,0,2:T(8,128)S...) while((s32[]{:T(128)}, f32[256,256]{1,0:T(8,128)S(1)}, ...), condition=%wide.wide.region_5.6_spmd.clone, body=%wide.wide.region_2.5_spmd.clone.sunk | while | flops 118861328 | bytes 6383152 | solution.py:115
  166.6 0.9 fusion.192
  174.8 0.9 fusion.192
  182.9 0.9 fusion.192
  191.1 0.9 fusion.192
  199.3 0.9 fusion.192
  207.4 0.9 fusion.192
  215.6 0.9 fusion.192
  223.7 0.9 fusion.192
  231.9 0.9 fusion.192
  240.1 0.9 fusion.192
  248.2 0.9 fusion.192
  256.4 0.9 fusion.192
  264.6 0.9 fusion.192
  272.7 0.9 fusion.192
  280.9 0.9 fusion.192
  289.1 0.9 fusion.192
  297.2 0.9 fusion.192
  305.4 0.9 fusion.192
  313.6 0.9 fusion.192
  321.7 0.9 fusion.192
  329.9 0.9 fusion.192
  338.0 0.9 fusion.192
  346.2 0.9 fusion.192
  350.7 0.9 bitcast_dynamic-update-slice_fusion.3
  354.4 0.9 fusion.192
  362.5 0.9 fusion.192
  370.7 0.9 fusion.192
  378.9 0.9 fusion.192
  387.0 0.9 fusion.192
  391.5 0.9 bitcast_dynamic-update-slice_fusion.3
  395.2 0.9 fusion.192
  403.4 0.9 fusion.192
  411.5 0.9 fusion.192
  419.7 0.9 fusion.192
  423.7 33.2 %reduce-scatter.5.cloned.1.call-done = f32[32,256]{1,0:T(8,128)} async-done(((f32[256,256]{1,0:T(8,128)}), f32[32,256]{1,0:T(8,128)}) %reduce-scatter.5.cloned.1.call-update) | async-done | bytes 32784 | tf_op jit(solution)/shard_map/reduce_scatter | solution.py:161
  456.9 37.8 %reduce-scatter.3.cloned.1.call-done = f32[32,256]{1,0:T(8,128)} async-done(((f32[256,256]{1,0:T(8,128)}), f32[32,256]{1,0:T(8,128)}) %reduce-scatter.3.cloned.1.call-update) | async-done | bytes 32784 | tf_op jit(solution)/shard_map/reduce_scatter | solution.py:160
  494.7 1.4 divide_bitcast_fusion
  (1183 shorter events, 230.2 us)
Async XLA Ops:
  10.4 27.9 %all-to-all-start.1 = ((s32[64,4,2]{1,2,0:T(2,128)}), s32[64,4,2]{1,2,0:T(2,128)S(1)}, u32[]{:S(2)}, u32[]{:S(2)}) async-start(s32[64,4,2]{1,2,0:T(2,128)} %copy.93), calls=%async_computation.1 | async-start | bytes 131072 | tf_op jit(solution)/shard_map/all_to_all | solution.py:151
  31.2 12.9 %copy-start.4 = (bf16[1,128,64]{1,2,0:T(8,128)(2,1)S(1)}, bf16[1,128,64]{1,2,0:T(8,128)(2,1)}, u32[]{:S(2)}) copy-start(bf16[1,128,64]{1,2,0:T(8,128)(2,1)} %param.11) | copy-start | bytes 49156
  31.2 12.9 %copy-start.5 = (bf16[1,128,8]{1,2,0:T(8,128)(2,1)S(1)}, bf16[1,128,8]{1,2,0:T(8,128)(2,1)}, u32[]{:S(2)}) copy-start(bf16[1,128,8]{1,2,0:T(8,128)(2,1)} %param.13) | copy-start | bytes 6148
  31.2 12.9 %copy-start.6 = (bf16[1,128]{1,0:T(2,128)(2,1)S(1)}, bf16[1,128]{1,0:T(2,128)(2,1)}, u32[]{:S(2)}) copy-start(bf16[1,128]{1,0:T(2,128)(2,1)} %param.14) | copy-start | bytes 772
  31.2 76.7 %copy-start.3 = (bf16[1,1,21,21]{3,2,1,0:T(8,128)(2,1)S(1)}, bf16[1,1,21,21]{3,2,1,0:T(8,128)(2,1)}, u32[]{:S(2)}) copy-start(bf16[1,1,21,21]{3,2,1,0:T(8,128)(2,1)} %param.12) | copy-start | bytes 2650
  38.3 57.0 %all-to-all-start.2 = ((bf16[64,4,4096]{2,1,0:T(4,128)(2,1)}), bf16[64,4,4096]{2,1,0:T(4,128)(2,1)S(1)}, u32[]{:S(2)}, u32[]{:S(2)}) async-start(bf16[64,4,4096]{2,1,0:T(4,128)(2,1)} %reshape.221), calls=%async_computation.2 | async-start | bytes 4194304 | tf_op jit(solution)/shard_map/all_to_all | solution.py:149
  95.3 65.7 %all-to-all-start = ((bf16[64,4,73]{2,1,0:T(4,128)(2,1)}), bf16[64,4,73]{2,1,0:T(4,128)(2,1)S(1)}, u32[]{:S(2)}, u32[]{:S(2)}) async-start(bf16[64,4,73]{2,1,0:T(4,128)(2,1)} %bitcast.4), calls=%async_computation | async-start | bytes 131072 | tf_op jit(solution)/shard_map/all_to_all | solution.py:150
  107.8 349.1 %reduce-scatter.5.cloned.1.call-start = ((), (), s32[]{:S(2)}) async-start(), calls=%async_computation.6 | async-start | bytes 294912 | tf_op jit(solution)/shard_map/reduce_scatter | solution.py:161
  157.6 3.4 copy-start.1
  422.3 0.7 copy-start
  422.3 0.8 copy-start.2
  423.0 71.7 %reduce-scatter.3.cloned.1.call-start = ((), (), s32[]{:S(2)}) async-start(), calls=%async_computation.5 | async-start | bytes 294912 | tf_op jit(solution)/shard_map/reduce_scatter | solution.py:160
Sparse Core Ops, SparseCore 0:
  423.1 33.7 reduce-scatter.4
  459.9 34.7 reduce-scatter.2
where the time goes:
time: 506 us; the launch traced here: 503 us
  local copies, waits for them, and re-layouts  135 us (27%)
  waiting for transfers between devices  129 us (25%)
  matrix products  91.7 us (18%)
  blocking collectives  49.5 us (10%)
  other arithmetic  42.5 us (8%)
  starting transfers between devices  34.9 us (7%)
  between operations  14.2 us (3%)
  loops' own time  5.66 us (1%)
    while x640, local copies, waits for them, and re-layouts  88.1 us
    all_to_all x1, waiting for transfers between devices, per_device(): lax.all_to_all(packed_pixels, 'patch', split_axis=0, concat_axis=0, tiled...  50.3 us
    all_gather x1, blocking collectives, per_device(): full_basis = lax.all_gather(basis[0], 'patch', axis=0, tiled=True)  49.5 us
    reduce_scatter x1, waiting for transfers between devices, per_device(): lax.psum_scatter(numerator, 'visit', scatter_dimension=0, tiled=True)  37.8 us
    reduce_scatter x1, waiting for transfers between devices, per_device(): lax.psum_scatter(depth_map, 'visit', scatter_dimension=0, tiled=True)  33.2 us
    dot_general x32, matrix products, update(): jnp.einsum('nri,nic->rc', row_map, spread, preferred_element_type=jnp.flo...  28.8 us
    reduce_sum x32, other arithmetic, update(): column_weight = jnp.sum(column_map.astype(jnp.float32), axis=2)  27.4 us
    squeeze x32, local copies, waits for them, and re-layouts, accumulate(): final_state, unused = lax.scan(update, initial, blocks)  27.1 us
  transfers between devices with their start and end apart: 5, of which 4 were waited for; matrix products, arithmetic and copies ran while one was open for 2% of the time, Pallas kernels for 0%

commit v1 on v0

--- a/solution.py
+++ b/solution.py
@@ -122,7 +122,9 @@
     height = stamps.shape[2]
     breadth = stamps.shape[3]
     slot_count = 2 * stamp_count // peer_count
-    full_basis = lax.all_gather(basis[0], "patch", axis=0, tiled=True)
+    full_basis = jnp.concatenate(
+        lax.all_to_all(jnp.stack([basis[0]] * lax.axis_size("patch")), "patch", 0, 0), axis=0
+    )
     destination = target[0, :, 0]
     position = jnp.arange(stamp_count, dtype=jnp.int32)
     earlier = (destination[None, :] == destination[:, None]) & (

time: 506 us -> 481 us (0.951)
  blocking collectives: 49.5 us -> 27.7 us
  starting transfers between devices: 34.9 us -> 24.4 us
  waiting for transfers between devices: 129 us -> 135 us
    all_gather x1 -> x0, blocking collectives: 49.5 us -> none  [per_device(): full_basis = lax.all_gather(basis[0], 'patch', axis=0, tiled=True)]
    all_to_all x0 -> x1, blocking collectives: none -> 27.7 us  [per_device(): lax.all_to_all(packed_starts, 'patch', split_axis=0, concat_axis=0, tiled...]
    all_to_all x1, starting transfers between devices: 16.6 us -> 5.53 us  [per_device(): lax.all_to_all(jnp.stack([basis[0]] * lax.axis_size('patch')), 'patch', 0...]
    all_to_all x1, waiting for transfers between devices: 0.01 us -> 7.61 us  [per_device(): lax.all_to_all(packed_extras, 'patch', split_axis=0, concat_axis=0, tiled...]
  transfers between devices with their start and end apart: 5 -> 5, of which waited for: 4 -> 5; matrix products, arithmetic and copies ran while one was open for 2% -> 2% of each run, Pallas kernels for 0% -> 0%
where the time goes in v1:
time: 481 us; the launch traced here: 477 us
  local copies, waits for them, and re-layouts  136 us (28%)
  waiting for transfers between devices  135 us (28%)
  matrix products  91.7 us (19%)
  other arithmetic  42.5 us (9%)
  blocking collectives  27.7 us (6%)
  starting transfers between devices  24.4 us (5%)
  between operations  14.2 us (3%)
  loops' own time  5.66 us (1%)
    while x640, local copies, waits for them, and re-layouts  88.1 us
    all_to_all x1, waiting for transfers between devices, per_device(): lax.all_to_all(packed_pixels, 'patch', split_axis=0, concat_axis=0, tiled...  49.8 us
    reduce_scatter x1, waiting for transfers between devices, per_device(): lax.psum_scatter(numerator, 'visit', scatter_dimension=0, tiled=True)  37.8 us
    dot_general x32, matrix products, update(): jnp.einsum('nri,nic->rc', row_map, spread, preferred_element_type=jnp.flo...  28.8 us
    reduce_scatter x1, waiting for transfers between devices, per_device(): lax.psum_scatter(depth_map, 'visit', scatter_dimension=0, tiled=True)  28.3 us
    all_to_all x1, blocking collectives, per_device(): lax.all_to_all(packed_starts, 'patch', split_axis=0, concat_axis=0, tiled...  27.7 us
    reduce_sum x32, other arithmetic, update(): column_weight = jnp.sum(column_map.astype(jnp.float32), axis=2)  27.4 us
    squeeze x32, local copies, waits for them, and re-layouts, accumulate(): final_state, unused = lax.scan(update, initial, blocks)  27.1 us
  transfers between devices with their start and end apart: 5, of which 5 were waited for; matrix products, arithmetic and copies ran while one was open for 2% of the time, Pallas kernels for 0%

profile of v1, /device:TPU:8, one launch (start us, length us, event | category | flops | bytes accessed | tf_op | source)
XLA Modules:
  0.0 477.1 jit_solution(18073246285722644775)
XLA Ops:
  7.2 0.9 convert_reduce_fusion.2
  9.8 27.7 %all_to_all.20 = s32[64,4,2]{1,2,0:T(2,128)S(1)} all-to-all(s32[64,4,2]{1,2,0:T(2,128)S(1)} %copy.90), channel_id=1, replica_groups=mesh['patch'=64,'visit'=8] {'patch'}, dimensions={0} | all-to-all | bytes 4096 | tf_op jit(solution)/shard_map/all_to_all | solution.py:153
  37.5 1.5 stack.139
  38.9 5.5 %all-to-all-start.2 = ((bf16[64,1,21,21]{3,2,1,0:T(8,128)(2,1)}), bf16[64,1,21,21]{3,2,1,0:T(8,128)(2,1)S(1)}, u32[]{:S(2)}, u32[]{:S(2)}) async-start(bf16[64,1,21,21]{3,2,1,0:T(8,128)(2,1)} %stack.139), calls=%async_computation.2 | async-start | bytes 786432 | tf_op jit(solution)/shard_map/all_to_all | solution.py:126
  44.5 2.0 convolution_convert_fusion.3
  46.4 2.2 reshape.218
  48.7 10.6 %all-to-all-done.2 = bf16[64,1,21,21]{3,2,1,0:T(8,128)(2,1)S(1)} async-done(((bf16[64,1,21,21]{3,2,1,0:T(8,128)(2,1)}), bf16[64,1,21,21]{3,2,1,0:T(8,128)(2,1)S(1)}, u32[]{:S(2)}, u32[]{:S(2)}) %all-to-all-start.2) | async-done | bytes 56480 | tf_op jit(solution)/shard_map/all_to_all | solution.py:126
  59.3 6.0 %all-to-all-start.3 = ((bf16[64,4,4096]{2,1,0:T(4,128)(2,1)}), bf16[64,4,4096]{2,1,0:T(4,128)(2,1)S(1)}, u32[]{:S(2)}, u32[]{:S(2)}) async-start(bf16[64,4,4096]{2,1,0:T(4,128)(2,1)} %reshape.218), calls=%async_computation.3 | async-start | bytes 4194304 | tf_op jit(solution)/shard_map/all_to_all | solution.py:151
  66.2 49.8 %all-to-all-done.3 = bf16[64,4,4096]{2,1,0:T(4,128)(2,1)S(1)} async-done(((bf16[64,4,4096]{2,1,0:T(4,128)(2,1)}), bf16[64,4,4096]{2,1,0:T(4,128)(2,1)S(1)}, u32[]{:S(2)}, u32[]{:S(2)}) %all-to-all-start.3) | async-done | bytes 2097184 | tf_op jit(solution)/shard_map/all_to_all | solution.py:151
  116.0 12.7 %all-to-all-start = ((bf16[64,4,73]{2,1,0:T(4,128)(2,1)}), bf16[64,4,73]{2,1,0:T(4,128)(2,1)S(1)}, u32[]{:S(2)}, u32[]{:S(2)}) async-start(bf16[64,4,73]{2,1,0:T(4,128)(2,1)} %bitcast.4), calls=%async_computation | async-start | bytes 131072 | tf_op jit(solution)/shard_map/all_to_all | solution.py:152
  129.2 3.2 reshape_reshape.17
  132.5 7.6 %all-to-all-done = bf16[64,4,73]{2,1,0:T(4,128)(2,1)S(1)} async-done(((bf16[64,4,73]{2,1,0:T(4,128)(2,1)}), bf16[64,4,73]{2,1,0:T(4,128)(2,1)S(1)}, u32[]{:S(2)}, u32[]{:S(2)}) %all-to-all-start) | async-done | bytes 37408 | tf_op jit(solution)/shard_map/all_to_all | solution.py:152
  140.1 261.2 %while.16 = (s32[]{:T(128)}, f32[256,256]{1,0:T(8,128)S(1)}, f32[256,256]{1,0:T(8,128)S(1)}, bf16[32,8,73]{2,1,0:T(8,128)(2,1)S(1)}, s32[32,8,2]{1,0,2:T(8,128)S...) while((s32[]{:T(128)}, f32[256,256]{1,0:T(8,128)S(1)}, ...), condition=%wide.wide.region_5.6_spmd.clone, body=%wide.wide.region_2.5_spmd.clone.sunk | while | flops 118861328 | bytes 6383152 | solution.py:115
  145.7 0.9 fusion.192
  153.8 0.9 fusion.192
  162.0 0.9 fusion.192
  170.2 0.9 fusion.192
  178.3 0.9 fusion.192
  186.5 0.9 fusion.192
  194.7 0.9 fusion.192
  202.8 0.9 fusion.192
  211.0 0.9 fusion.192
  219.2 0.9 fusion.192
  227.3 0.9 fusion.192
  235.5 0.9 fusion.192
  243.7 0.9 fusion.192
  251.8 0.9 fusion.192
  260.0 0.9 fusion.192
  268.1 0.9 fusion.192
  276.3 0.9 fusion.192
  284.5 0.9 fusion.192
  292.6 0.9 fusion.192
  300.8 0.9 fusion.192
  309.0 0.9 fusion.192
  317.1 0.9 fusion.192
  325.3 0.9 fusion.192
  333.5 0.9 fusion.192
  341.6 0.9 fusion.192
  349.8 0.9 fusion.192
  358.0 0.9 fusion.192
  366.1 0.9 fusion.192
  374.3 0.9 fusion.192
  382.4 0.9 fusion.192
  390.6 0.9 fusion.192
  398.8 0.9 fusion.192
  402.8 28.3 %reduce-scatter.5.cloned.1.call-done = f32[32,256]{1,0:T(8,128)} async-done(((f32[256,256]{1,0:T(8,128)}), f32[32,256]{1,0:T(8,128)}) %reduce-scatter.5.cloned.1.call-update) | async-done | bytes 32784 | tf_op jit(solution)/shard_map/reduce_scatter | solution.py:163
  431.1 37.8 %reduce-scatter.3.cloned.1.call-done = f32[32,256]{1,0:T(8,128)} async-done(((f32[256,256]{1,0:T(8,128)}), f32[32,256]{1,0:T(8,128)}) %reduce-scatter.3.cloned.1.call-update) | async-done | bytes 32784 | tf_op jit(solution)/shard_map/reduce_scatter | solution.py:162
  468.9 1.4 divide_bitcast_fusion
  (1182 shorter events, 231.3 us)
Async XLA Ops:
  38.9 20.3 %all-to-all-start.2 = ((bf16[64,1,21,21]{3,2,1,0:T(8,128)(2,1)}), bf16[64,1,21,21]{3,2,1,0:T(8,128)(2,1)S(1)}, u32[]{:S(2)}, u32[]{:S(2)}) async-start(bf16[64,1,21,21]{3,2,1,0:T(8,128)(2,1)} %stack.139), calls=%async_computation.2 | async-start | bytes 786432 | tf_op jit(solution)/shard_map/all_to_all | solution.py:126
  48.7 16.6 %copy-start.3 = (bf16[1,128,64]{1,2,0:T(8,128)(2,1)S(1)}, bf16[1,128,64]{1,2,0:T(8,128)(2,1)}, u32[]{:S(2)}) copy-start(bf16[1,128,64]{1,2,0:T(8,128)(2,1)} %param.11) | copy-start | bytes 49156
  48.7 16.6 %copy-start.4 = (bf16[1,128,8]{1,2,0:T(8,128)(2,1)S(1)}, bf16[1,128,8]{1,2,0:T(8,128)(2,1)}, u32[]{:S(2)}) copy-start(bf16[1,128,8]{1,2,0:T(8,128)(2,1)} %param.13) | copy-start | bytes 6148
  48.7 16.6 %copy-start.5 = (bf16[1,128]{1,0:T(2,128)(2,1)S(1)}, bf16[1,128]{1,0:T(2,128)(2,1)}, u32[]{:S(2)}) copy-start(bf16[1,128]{1,0:T(2,128)(2,1)} %param.14) | copy-start | bytes 772
  59.3 56.7 %all-to-all-start.3 = ((bf16[64,4,4096]{2,1,0:T(4,128)(2,1)}), bf16[64,4,4096]{2,1,0:T(4,128)(2,1)S(1)}, u32[]{:S(2)}, u32[]{:S(2)}) async-start(bf16[64,4,4096]{2,1,0:T(4,128)(2,1)} %reshape.218), calls=%async_computation.3 | async-start | bytes 4194304 | tf_op jit(solution)/shard_map/all_to_all | solution.py:151
  116.0 24.1 %all-to-all-start = ((bf16[64,4,73]{2,1,0:T(4,128)(2,1)}), bf16[64,4,73]{2,1,0:T(4,128)(2,1)S(1)}, u32[]{:S(2)}, u32[]{:S(2)}) async-start(bf16[64,4,73]{2,1,0:T(4,128)(2,1)} %bitcast.4), calls=%async_computation | async-start | bytes 131072 | tf_op jit(solution)/shard_map/all_to_all | solution.py:152
  128.7 302.4 %reduce-scatter.5.cloned.1.call-start = ((), (), s32[]{:S(2)}) async-start(), calls=%async_computation.7 | async-start | bytes 294912 | tf_op jit(solution)/shard_map/reduce_scatter | solution.py:163
  129.2 3.3 copy-start.1
  401.3 0.7 copy-start
  401.4 0.8 copy-start.2
  402.1 66.8 %reduce-scatter.3.cloned.1.call-start = ((), (), s32[]{:S(2)}) async-start(), calls=%async_computation.6 | async-start | bytes 294912 | tf_op jit(solution)/shard_map/reduce_scatter | solution.py:162
Sparse Core Ops, SparseCore 0:
  402.2 28.8 reduce-scatter.4
  434.1 34.7 reduce-scatter.2
